TPU v7x, 32 devices: a whole 2x2x4 slice. The times are simulated.
32 devices in a mesh: dp: 8 (over z, y), tensor: 4 (over x, core).
Axes of the slice: x: 2, y: 2, z: 4, core: 2. Of those that a mesh axis runs over, the one named last changes fastest.
Arguments:
- tokens: bfloat16 [2, 128, 12288], P(None, 'dp', 'tensor'), may hold values from -6 to 6
- up_weight: bfloat16 [12288, 49152], P('tensor', 'dp'), may hold values from -0.0546875 to 0.0546875
- up_bias: bfloat16 [49152], P('dp'), may hold values from -3 to 3
- down_weight: bfloat16 [49152, 12288], P('dp', 'tensor'), may hold values from -0.02734375 to 0.02734375
- down_bias: bfloat16 [12288], P('tensor'), may hold values from -3 to 3
- active: int32 [2, 1, 384], P(None, None, 'dp'), may hold values from 0 to 1
Outputs:
- mixed: bfloat16 [2, 128, 12288], P(None, 'dp', 'tensor')
All inputs are finite; a program needn't handle non-finite values.
Results may differ from a plain program's by a relative error of at most 0.0042.
Values may be sent and summed in bfloat16 or wider, within the bound.
A program may use at most 128 MiB of HBM per device.

v0:
```python
import functools

import jax
import jax.numpy as jnp
from jax import lax
from jax.experimental import pallas as pl
from jax.experimental.pallas import tpu as pltpu
from jax.sharding import PartitionSpec as P

RBLK = 128
TILE = 512
LAG = 3
MESH = pl.DeviceIdType.MESH


def activate(summed, up_bias, mask_table, first_row):
    row_count = summed.shape[0]
    blocks = mask_table.shape[1]
    row_ids = first_row + jnp.arange(row_count, dtype=jnp.int32)
    onehot = (
        row_ids[:, None] // RBLK == jnp.arange(mask_table.shape[0], dtype=jnp.int32)[None, :]
    ).astype(jnp.float32)
    row_mask = jnp.dot(onehot, mask_table.astype(jnp.float32))
    preact = jnp.maximum(summed + up_bias.astype(jnp.float32), 0.0)
    gated_rows = preact.reshape(row_count, blocks, -1) * row_mask[:, :, None]
    return gated_rows.reshape(row_count, -1).astype(jnp.bfloat16)


def local(tokens, up_weight, up_bias, down_weight, down_bias, active):
    results = []
    for step_index in range(tokens.shape[0]):
        local_rows = tokens[step_index]
        mask_table = active[step_index]
        partial_up = jnp.dot(
            lax.all_gather(local_rows, "dp", axis=0, tiled=True),
            up_weight,
            preferred_element_type=jnp.float32,
        )
        row_share = lax.psum_scatter(partial_up, "tensor", scatter_dimension=0, tiled=True)
        first_row = lax.axis_index("tensor") * row_share.shape[0]
        hidden_share = activate(row_share, up_bias, mask_table, first_row)
        hidden = lax.all_gather(hidden_share, "tensor", axis=0, tiled=True)
        mixed_rows = lax.psum_scatter(
            jnp.dot(hidden, down_weight, preferred_element_type=jnp.float32),
            "dp",
            scatter_dimension=0,
            tiled=True,
        )
        results.append((mixed_rows + down_bias.astype(jnp.float32)).astype(jnp.bfloat16))
    return jnp.stack(results)


def fused_kernel(nz, nt, tok, wu, wd, bias_u, active, out,
                 x_all, w, pbuf, crecv, xsend, xrecv, hid, acc, ysend, yrecv, zsend, zrecv,
                 tsem, wsem, ag_send, ag_recv, c_send, c_recv, x_send, x_recv, h_send, h_recv,
                 y_send, y_recv, z_send, z_recv):
    f32, bf16 = jnp.float32, jnp.bfloat16
    steps, share, depth = tok.shape
    rows = x_all.shape[1]
    half = rows // 2
    dp, t = lax.axis_index("dp"), lax.axis_index("tensor")
    z, y = dp // 2, dp % 2
    x, c = t // 2, t % 2
    y_peer = (z * 2 + 1 - y, t)
    x_peer = (dp, (1 - x) * 2 + c)
    c_peer = (dp, x * 2 + 1 - c)
    z_of = lambda k: lax.rem(z + k, nz)
    own = pl.ds(pl.multiple_of(c * half, half), half)
    other = pl.ds(pl.multiple_of((1 - c) * half, half), half)
    cols = lambda j: pl.ds(pl.multiple_of(j * TILE, TILE), TILE)
    nc = depth // TILE
    spans = nt // nc
    block = lambda d: pl.ds(pl.multiple_of(d * share, share), share)

    def rcopy(src, dst, ss, rs, dev):
        return pltpu.make_async_remote_copy(
            src_ref=src, dst_ref=dst, send_sem=ss, recv_sem=rs, device_id=dev, device_id_type=MESH
        )

    def up_load(j):
        return pltpu.make_async_copy(wu.at[:, cols(j)], w.at[j], wsem.at[j])

    def down_load(i):
        n, part = i // spans, i % spans
        lines = pl.ds(pl.multiple_of(part * depth, depth), depth)
        return pltpu.make_async_copy(wd.at[lines, cols(n)], w.at[i], wsem.at[i])

    mine = [pltpu.make_async_copy(tok.at[s], x_all.at[s, block(dp)], tsem.at[s]) for s in range(steps)]
    for copy in mine:
        copy.start()

    @pl.loop(0, nt)
    def _(j):
        up_load(j).start()

    barrier = pltpu.get_barrier_semaphore()
    peers = [y_peer, x_peer, c_peer] + [(z_of(k) * 2 + y, t) for k in range(1, nz)]
    for peer in peers:
        pl.semaphore_signal(barrier, inc=1, device_id=peer, device_id_type=MESH)
    pl.semaphore_wait(barrier, len(peers))

    def ag_copy(s, k, d, peer):
        view = x_all.at[s, block(d)]
        return rcopy(view, view, ag_send.at[s, k], ag_recv.at[s, d], peer)

    def ag_sends(s):
        mine[s].wait()
        ag_copy(s, 0, dp, y_peer).start()
        for k in range(1, nz):
            ag_copy(s, k, dp, (z_of(k) * 2 + y, t)).start()

    def ag_forward(s, k):
        d = z_of(k) * 2 + y
        ag_copy(s, k, d, y_peer).wait_recv()
        ag_copy(s, nz - 1 + k, d, y_peer).start()

    def ag_finish(s):
        for k in range(nz):
            ag_copy(s, k, z_of(k) * 2 + 1 - y, y_peer).wait_recv()

    def c_copy(q):
        return rcopy(pbuf.at[q, other], crecv.at[q], c_send.at[q], c_recv.at[q], c_peer)

    def x_copy(q):
        return rcopy(xsend.at[q], xrecv.at[q], x_send.at[q], x_recv.at[q], x_peer)

    def h_copy(s, j, lines):
        view, q = hid.at[s, lines, cols(j)], s * nt + j
        return rcopy(view, view, h_send.at[q], h_recv.at[q], c_peer)

    def up(s, j):
        q = s * nt + j
        pbuf[q] = jnp.dot(x_all[s], w[j], preferred_element_type=f32)
        c_copy(q).start()

    def mid(q):
        c_copy(q).wait_recv()
        total = pbuf[q, own] + crecv[q]
        crecv[q] = total
        xsend[q] = total.astype(bf16)
        x_copy(q).start()

    def act(s, j):
        q = s * nt + j
        x_copy(q).wait_recv()
        bias = bias_u[cols(j)].astype(f32).reshape(1, TILE)
        pre = jnp.maximum(crecv[q] + xrecv[q].astype(f32) + bias, 0.0)
        blocks = active.shape[2] // nt
        width = TILE // blocks
        for b in range(blocks):
            gate = active[s, 0, j * blocks + b].astype(f32)
            lanes = pl.ds(pl.multiple_of(j * TILE + b * width, width), width)
            hid[s, own, lanes] = (pre[:, b * width : (b + 1) * width] * gate).astype(bf16)
        h_copy(s, j, own).start()

    def hidden_ready(s):
        @pl.loop(0, nt)
        def _(j):
            h_copy(s, j, other).wait_recv()

    def y_copy(i):
        return rcopy(ysend.at[i], yrecv.at[i], y_send.at[i], y_recv.at[i], y_peer)

    def z_copy(i, k):
        q = i * nz + k
        return rcopy(zsend.at[q], zrecv.at[q], z_send.at[q], z_recv.at[q], (z_of(k) * 2 + y, t))

    def down(s, n):
        total = jnp.zeros((rows, TILE), f32)
        for part in range(spans):
            total += jnp.dot(
                hid[s, :, part * depth : (part + 1) * depth], w[n * spans + part], preferred_element_type=f32
            )
        acc[s, :, cols(n)] = total
        i = s * nc + n
        for zz in range(nz):
            ysend[i, zz] = acc[s, block(zz * 2 + 1 - y), cols(n)].astype(bf16)
        y_copy(i).start()

    def rs_z(s, n):
        i = s * nc + n
        y_copy(i).wait_recv()
        for k in range(1, nz):
            pair = acc[s, block(z_of(k) * 2 + y), cols(n)] + yrecv[i, z_of(k)].astype(f32)
            zsend[i * nz + k] = pair.astype(bf16)
            z_copy(i, k).start()

    def rs_finish(s, n):
        i = s * nc + n
        total = acc[s, block(dp), cols(n)] + yrecv[i, z].astype(f32)
        for k in range(1, nz):
            z_copy(i, k).wait_recv()
            total += zrecv[i * nz + k].astype(f32)
        out[s, :, cols(n)] = total

    ag_sends(0)
    for k in range(1, nz):
        ag_forward(0, k)
    ag_sends(1)
    ag_finish(0)

    def first_step(j):
        up_load(j).wait()
        up(0, j)

        @pl.when(j >= 1)
        def _():
            mid(j - 1)

    cut = [nt * k // (nz + 1) for k in range(nz)] + [nt]
    for k in range(nz):
        pl.loop(cut[k], cut[k + 1])(first_step)
        if k + 1 < nz:
            ag_forward(1, k + 1)
    mid(nt - 1)
    ag_finish(1)

    @pl.loop(0, nt)
    def _(j):
        up(1, j)

        @pl.when(j >= 1)
        def _():
            mid(nt + j - 1)
            down_load(j - 1).start()

        act(0, j)

    mid(2 * nt - 1)
    down_load(nt - 1).start()
    hidden_ready(0)

    @pl.loop(0, nc)
    def _(n):
        for part in range(spans):
            down_load(n * spans + part).wait()
        down(0, n)

        @pl.when(n >= LAG)
        def _():
            rs_z(0, n - LAG)

    @pl.loop(0, nt // 2)
    def _(j):
        act(1, j)

    @pl.loop(nc - LAG, nc)
    def _(n):
        rs_z(0, n)

    @pl.loop(nt // 2, nt)
    def _(j):
        act(1, j)

    hidden_ready(1)

    @pl.loop(0, nc)
    def _(n):
        down(1, n)

        @pl.when(n >= LAG)
        def _():
            rs_z(1, n - LAG)

    @pl.loop(nc - LAG, nc)
    def _(n):
        rs_z(1, n)

    for s in range(steps):
        @pl.loop(0, nc)
        def _(n):
            rs_finish(s, n)

    for s in range(steps):
        for k in range(2 * nz - 1):
            ag_copy(s, k, dp, y_peer).wait_send()

    @pl.loop(0, steps * nc)
    def _(i):
        y_copy(i).wait_send()
        for k in range(1, nz):
            z_copy(i, k).wait_send()

    for s in range(steps):
        @pl.loop(0, nt)
        def _(j):
            c_copy(s * nt + j).wait_send()
            x_copy(s * nt + j).wait_send()
            h_copy(s, j, own).wait_send()


def fused(groups, tokens, up_weight, up_bias, down_weight, down_bias, active):
    steps, share, depth = tokens.shape
    hidden = up_weight.shape[1]
    rows, nz, nt, nc = groups * share, groups // 2, hidden // TILE, depth // TILE
    f32, bf16 = jnp.float32, jnp.bfloat16
    any_space, vmem = pl.BlockSpec(memory_space=pl.ANY), pl.BlockSpec(memory_space=pltpu.VMEM)
    smem = pl.BlockSpec(memory_space=pltpu.SMEM)
    dma = pltpu.SemaphoreType.DMA
    half = rows // 2
    mixed = pl.pallas_call(
        functools.partial(fused_kernel, nz, nt),
        out_shape=jax.ShapeDtypeStruct(tokens.shape, f32),
        in_specs=[any_space, any_space, any_space, vmem, smem],
        out_specs=vmem,
        scratch_shapes=[
            pltpu.VMEM((steps, rows, depth), bf16),
            pltpu.VMEM((nt, depth, TILE), bf16),
            pltpu.VMEM((steps * nt, rows, TILE), f32),
            pltpu.VMEM((steps * nt, half, TILE), f32),
            pltpu.VMEM((steps * nt, half, TILE), bf16),
            pltpu.VMEM((steps * nt, half, TILE), bf16),
            pltpu.VMEM((steps, rows, hidden), bf16),
            pltpu.VMEM((steps, rows, depth), f32),
        ]
        + [pltpu.VMEM((steps * nc, nz, share, TILE), bf16)] * 2
        + [pltpu.VMEM((steps * nc * nz, share, TILE), bf16)] * 2
        + [
            dma((steps,)),
            dma((nt,)),
            dma((steps, 2 * nz - 1)),
            dma((steps, 2 * nz)),
        ]
        + [dma((steps * nt,))] * 6
        + [dma((steps * nc,))] * 2
        + [dma((steps * nc * nz,))] * 2,
        compiler_params=pltpu.CompilerParams(
            collective_id=0, has_side_effects=True, vmem_limit_bytes=67043328
        ),
    )(tokens, up_weight, down_weight, up_bias, active)
    return (mixed + down_bias.astype(f32)).astype(bf16)


def solution(mesh):
    placed = (
        P(None, "dp", "tensor"),
        P("tensor", "dp"),
        P("dp"),
        P("dp", "tensor"),
        P("tensor"),
        P(None, None, "dp"),
    )
    groups, columns = mesh.shape["dp"], mesh.shape["tensor"]

    def body(*args):
        steps, share, depth = args[0].shape
        hidden, table = args[1].shape[1], args[5].shape
        if (
            (groups, columns, steps, table[1]) == (8, 4, 2, 1)
            and share % 16 == 0
            and depth % TILE == 0
            and hidden % depth == 0
            and (hidden // TILE) and table[2] % (hidden // TILE) == 0
            and depth // TILE > LAG
        ):
            return fused(groups, *args)
        return local(*args)

    return jax.shard_map(
        body, mesh=mesh, in_specs=placed, out_specs=P(None, "dp", "tensor"), check_vma=False
    )
```

profile of v0, /device:TPU:0, one launch (start us, length us, event | category | flops | bytes accessed | tf_op | source)
XLA Modules:
  0.0 83.9 jit_solution(16933659365572903243)
XLA Ops:
  0.0 1.3 %convert_element_type.6 = f32[3072]{0:T(1024)} convert(bf16[3072]{0:T(1024)(128)(2,1)} %param.10) | non-fusion elementwise | flops 3072 | bytes 18432 | tf_op jit(solution)/shard_map/convert_element_type | solution.py:331
  1.3 80.9 %shard_map.64 = f32[2,16,3072]{2,1,0:T(8,128)} custom-call(bf16[2,16,3072]{2,1,0:T(8,128)(2,1)} %tok.1, bf16[3072,6144]{1,0:T(8,128)(2,1)} %wu.1, bf16[6144,3072]{1,0:T(8,128)(2,1)} %wd.1, bf16[6144]{0:T(1024)(128)(2,1)} %bias_u.1, s32[2,1,48]{2,1,0:T(1,128)} %active.1), custom_call_target="tpu_custom_call" | custom-call | tf_op jit(solution)/shard_map/pallas_call | solution.py:301
  82.2 1.7 %add_convert_fusion = bf16[2,16,3072]{2,1,0:T(8,128)(2,1)} fusion(f32[2,16,3072]{2,1,0:T(8,128)} %shard_map.64, f32[3072]{0:T(1024)} %convert_element_type.6), kind=kLoop, calls=%fused_computation | loop fusion | flops 196608 | bytes 602112 | tf_op jit(solution)/shard_map/convert_element_type | solution.py:331
where the time goes:
time: 84.2 us; the launch traced here: 83.9 us
  Pallas kernels  80.9 us (96%)
  other arithmetic  2.99 us (4%)
    pallas_call x1, Pallas kernels, fused(): pl.pallas_call(functools.partial(fused_kernel, nz, nt), out_shape=jax.Sha...  80.9 us
    convert_element_type x2, other arithmetic, fused(): return (mixed + down_bias.astype(f32)).astype(bf16)  2.99 us

commit v1 on v0

v1 whole, which is shorter than its diff:
```python
import functools

import jax
import jax.numpy as jnp
from jax import lax
from jax.experimental import pallas as pl
from jax.experimental.pallas import tpu as pltpu
from jax.sharding import PartitionSpec as P

RBLK = 128
TILE = 512
LAG = 3
MESH = pl.DeviceIdType.MESH


def activate(summed, up_bias, mask_table, first_row):
    row_count = summed.shape[0]
    blocks = mask_table.shape[1]
    row_ids = first_row + jnp.arange(row_count, dtype=jnp.int32)
    onehot = (
        row_ids[:, None] // RBLK == jnp.arange(mask_table.shape[0], dtype=jnp.int32)[None, :]
    ).astype(jnp.float32)
    row_mask = jnp.dot(onehot, mask_table.astype(jnp.float32))
    preact = jnp.maximum(summed + up_bias.astype(jnp.float32), 0.0)
    gated_rows = preact.reshape(row_count, blocks, -1) * row_mask[:, :, None]
    return gated_rows.reshape(row_count, -1).astype(jnp.bfloat16)


def local(tokens, up_weight, up_bias, down_weight, down_bias, active):
    results = []
    for step_index in range(tokens.shape[0]):
        local_rows = tokens[step_index]
        mask_table = active[step_index]
        partial_up = jnp.dot(
            lax.all_gather(local_rows, "dp", axis=0, tiled=True),
            up_weight,
            preferred_element_type=jnp.float32,
        )
        row_share = lax.psum_scatter(partial_up, "tensor", scatter_dimension=0, tiled=True)
        first_row = lax.axis_index("tensor") * row_share.shape[0]
        hidden_share = activate(row_share, up_bias, mask_table, first_row)
        hidden = lax.all_gather(hidden_share, "tensor", axis=0, tiled=True)
        mixed_rows = lax.psum_scatter(
            jnp.dot(hidden, down_weight, preferred_element_type=jnp.float32),
            "dp",
            scatter_dimension=0,
            tiled=True,
        )
        results.append((mixed_rows + down_bias.astype(jnp.float32)).astype(jnp.bfloat16))
    return jnp.stack(results)


ORDER = (
    (0, 0, 1), (0, 0, 0), (0, 1, 0), (1, 0, 0),
    (1, 1, 0), (2, 0, 0), (2, 1, 0), (3, 0, 0),
    (3, 1, 0), (3, 0, 1), (3, 1, 1),
    (0, 1, 1), (1, 0, 1), (1, 1, 1), (2, 0, 1), (2, 1, 1),
)
SLOT = {key: i for i, key in enumerate(ORDER)}
CHUNKS = ((0, 4), (4, 8), (8, 16))
PARTS = ((0, 4), (4, 8), (8, 11), (11, 16))
PAIRS = (
    ((0, 0), (1, 0), (2, 0), (3, 0), (3, 1)),
    ((0, 1), (1, 1), (2, 1)),
)
HOPS = (((1, 0, 1), (2, 1, 2), (3, 2, 4)), ((1, 0, 1), (2, 1, 2)))


def fused_kernel(nt, tok, wu, wd, bias_u, active, out,
                 x_all, w, pbuf, crecv, xsend, xrecv, hid, acc,
                 ysend0, yrecv0, ysend1, yrecv1, zsend0, zrecv0, zsend1, zrecv1,
                 tsem, wsem, ag_send, ag_recv, c_send, c_recv, x_send, x_recv, h_send, h_recv,
                 y_send, y_recv, z_send, z_recv):
    f32, bf16 = jnp.float32, jnp.bfloat16
    steps, share, depth = tok.shape
    ysend, yrecv, zsend, zrecv = (ysend0, ysend1), (yrecv0, yrecv1), (zsend0, zsend1), (zrecv0, zrecv1)
    half = TILE // 2
    dp, t = lax.axis_index("dp"), lax.axis_index("tensor")
    z, y = dp // 2, dp % 2
    x, c = t // 2, t % 2
    y_peer = (z * 2 + 1 - y, t)
    x_peer = (dp, (1 - x) * 2 + c)
    c_peer = (dp, x * 2 + 1 - c)
    z_peer = (None, ((z + 1 - 2 * (z % 2)) * 2 + y, t), (lax.rem(z + 2, 4) * 2 + y, t), ((3 - z) * 2 + y, t))
    cols = lambda j: pl.ds(pl.multiple_of(j * TILE, TILE), TILE)
    side = lambda j, h: pl.ds(pl.multiple_of(j * TILE + h * half, half), half)
    nc = depth // TILE
    rows_of = lambda span: pl.ds(span[0] * share, (span[1] - span[0]) * share)
    slot = lambda *key: pl.ds(SLOT[key] * share, share)

    def rcopy(src, dst, ss, rs, dev):
        return pltpu.make_async_remote_copy(
            src_ref=src, dst_ref=dst, send_sem=ss, recv_sem=rs, device_id=dev, device_id_type=MESH
        )

    def up_load(j):
        return pltpu.make_async_copy(wu.at[:, cols(j)], w.at[j], wsem.at[j])

    def down_load(i):
        n, part = i // 2, i % 2
        lines = pl.ds(pl.multiple_of(part * depth, depth), depth)
        return pltpu.make_async_copy(wd.at[lines, cols(n)], w.at[i], wsem.at[i])

    mine = [pltpu.make_async_copy(tok.at[s], x_all.at[slot(0, 0, s)], tsem.at[s]) for s in range(steps)]
    for copy in mine:
        copy.start()

    @pl.loop(0, nt)
    def _(j):
        up_load(j).start()

    barrier = pltpu.get_barrier_semaphore()
    peers = [y_peer, x_peer, c_peer] + list(z_peer[1:])
    for peer in peers:
        pl.semaphore_signal(barrier, inc=1, device_id=peer, device_id_type=MESH)
    pl.semaphore_wait(barrier, len(peers))

    def gather(kind, s):
        src, dst, dev = (
            ((0, 0), (0, 1), y_peer),
            ((0, 0), (1, 0), z_peer[1]),
            ((0, 0), (2, 0), z_peer[2]),
            ((1, 0), (1, 1), y_peer),
            ((2, 0), (3, 0), z_peer[1]),
            ((2, 0), (2, 1), y_peer),
            ((3, 0), (3, 1), y_peer),
        )[kind]
        return rcopy(
            x_all.at[slot(*src, s)], x_all.at[slot(*dst, s)], ag_send.at[s, kind], ag_recv.at[s, kind], dev
        )

    def c_copy(ch, j):
        rows = rows_of(CHUNKS[ch])
        q = ch * nt + j
        return rcopy(pbuf.at[j, 1 - c, rows], crecv.at[j, rows], c_send.at[q], c_recv.at[q], c_peer)

    def x_copy(part, j):
        rows = rows_of(PARTS[part])
        q = part * nt + j
        return rcopy(xsend.at[j, rows], xrecv.at[j, rows], x_send.at[q], x_recv.at[q], x_peer)

    def h_copy(part, j, h):
        view = hid.at[rows_of(PARTS[part]), side(j, h)]
        q = part * nt + j
        return rcopy(view, view, h_send.at[q], h_recv.at[q], c_peer)

    def up(ch, j):
        rows = rows_of(CHUNKS[ch])
        total = jnp.dot(x_all[rows], w[j], preferred_element_type=f32)
        for h in range(2):
            pbuf[j, h, rows] = total[:, h * half : (h + 1) * half]
        c_copy(ch, j).start()

    def mid(part, j):
        rows = rows_of(PARTS[part])
        total = pbuf[j, c, rows] + crecv[j, rows]
        crecv[j, rows] = total
        xsend[j, rows] = total.astype(bf16)
        x_copy(part, j).start()

    def act(part, j):
        first, last = PARTS[part]
        rows = rows_of(PARTS[part])
        x_copy(part, j).wait_recv()
        bias = bias_u[side(j, c)].astype(f32).reshape(1, half)
        pre = jnp.maximum(crecv[j, rows] + xrecv[j, rows].astype(f32) + bias, 0.0)
        blocks = active.shape[2] // nt
        width = TILE // blocks
        for b in range(blocks // 2):
            lanes = pl.ds(pl.multiple_of(j * TILE + c * half + b * width, width), width)
            gates = [active[s, 0, j * blocks + c * (blocks // 2) + b].astype(f32) for s in range(steps)]
            i = first
            while i < last:
                n = i
                while n < last and ORDER[n][2] == ORDER[i][2]:
                    n += 1
                piece = pre[(i - first) * share : (n - first) * share, b * width : (b + 1) * width]
                hid[pl.ds(i * share, (n - i) * share), lanes] = (piece * gates[ORDER[i][2]]).astype(bf16)
                i = n
        h_copy(part, j, c).start()

    def hidden_ready(part, start, stop):
        @pl.loop(start, stop)
        def _(j):
            h_copy(part, j, 1 - c).wait_recv()

    slots_of = [[i for key in PAIRS[g] for i in (SLOT[key[0], 0, key[1]], SLOT[key[0], 1, key[1]])] for g in range(2)]
    lines_of = [sorted(slots, key=lambda i: i or len(ORDER)) for slots in slots_of]

    def hidden_rows(g, part):
        span = slice(part * depth, (part + 1) * depth)
        ids = lines_of[g]
        if ids[-1] != 0:
            return hid[ids[0] * share : (ids[-1] + 1) * share, span]
        return jnp.concatenate([hid[ids[0] * share : (ids[-2] + 1) * share, span], hid[:share, span]], axis=0)

    def y_copy(g, n):
        q = g * nc + n
        return rcopy(ysend[g].at[n], yrecv[g].at[n], y_send.at[q], y_recv.at[q], y_peer)

    def z_copy(g, n, hop):
        k, first, last = HOPS[g][hop]
        span = pl.ds(first, last - first)
        q = (g * nc + n) * 3 + hop
        return rcopy(zsend[g].at[n, span], zrecv[g].at[n, span], z_send.at[q], z_recv.at[q], z_peer[k])

    def share_out(g, n, total):
        for p, (k, s) in enumerate(PAIRS[g]):
            for e in range(2):
                i = lines_of[g].index(SLOT[k, e, s]) * share
                if e:
                    ysend[g][n, p] = total[i : i + share].astype(bf16)
                else:
                    acc[slot(k, 0, s), cols(n)] = total[i : i + share]
        y_copy(g, n).start()

    def down(n):
        total = jnp.zeros((len(lines_of[0]) * share, TILE), f32)
        for part in range(2):
            total += jnp.dot(hidden_rows(0, part), w[n * 2 + part], preferred_element_type=f32)
        share_out(0, n, total)

    def down_first(n):
        total = jnp.dot(hidden_rows(1, 0), w[n * 2], preferred_element_type=f32)
        for i, line in enumerate(lines_of[1]):
            acc[pl.ds(line * share, share), cols(n)] = total[i * share : (i + 1) * share]

    def down_second(n):
        total = jnp.concatenate([acc[pl.ds(line * share, share), cols(n)] for line in lines_of[1]], axis=0)
        total += jnp.dot(hidden_rows(1, 1), w[n * 2 + 1], preferred_element_type=f32)
        share_out(1, n, total)

    def rs_z(g, n):
        y_copy(g, n).wait_recv()
        for p, (k, s) in enumerate(PAIRS[g]):
            if k:
                pair = acc[slot(k, 0, s), cols(n)] + yrecv[g][n, p].astype(f32)
                zsend[g][n, p - 1] = pair.astype(bf16)
        for hop in range(len(HOPS[g])):
            z_copy(g, n, hop).start()

    def rs_finish(n):
        for g in range(2):
            for hop in range(len(HOPS[g])):
                z_copy(g, n, hop).wait_recv()
        for s in range(steps):
            total = acc[slot(0, 0, s), cols(n)] + yrecv[s][n, 0].astype(f32)
            for g in range(2):
                for p, (k, step) in enumerate(PAIRS[g]):
                    if k and step == s:
                        total += zrecv[g][n, p - 1].astype(f32)
            out[s, :, cols(n)] = total

    for copy in mine:
        copy.wait()
    for s in (0, 1):
        gather(0, s).start()
        gather(1, s).start()
    gather(1, 0).wait_recv()
    gather(3, 0).start()
    gather(2, 0).start()
    gather(2, 1).start()
    gather(0, 0).wait_recv()

    def first_chunk(j):
        up_load(j).wait()
        up(0, j)

        @pl.when(j >= LAG)
        def _():
            c_copy(0, j - LAG).wait_recv()
            mid(0, j - LAG)

    def forward_far(s):
        gather(2, s).wait_recv()
        gather(4, s).start()
        gather(5, s).start()

    def forward_last(s):
        gather(4, s).wait_recv()
        gather(6, s).start()

    cut = [0, nt // 4, nt // 2, nt * 3 // 4, nt]
    pl.loop(cut[0], cut[1])(first_chunk)
    gather(1, 1).wait_recv()
    gather(3, 1).start()
    pl.loop(cut[1], cut[2])(first_chunk)
    forward_far(0)
    pl.loop(cut[2], cut[3])(first_chunk)
    forward_far(1)
    pl.loop(cut[3], cut[4])(first_chunk)
    forward_last(0)
    gather(3, 0).wait_recv()
    gather(5, 0).wait_recv()

    @pl.loop(0, LAG)
    def _(j):
        up(1, j)
        c_copy(0, nt - LAG + j).wait_recv()
        mid(0, nt - LAG + j)

    forward_last(1)

    @pl.loop(LAG, nt)
    def _(j):
        up(1, j)
        c_copy(1, j - LAG).wait_recv()
        mid(1, j - LAG)
        act(0, j - LAG)

    gather(6, 0).wait_recv()
    for kind in (0, 3, 5, 6):
        gather(kind, 1).wait_recv()

    @pl.loop(0, LAG)
    def _(j):
        up(2, j)
        down_load(j).start()
        c_copy(1, nt - LAG + j).wait_recv()
        mid(1, nt - LAG + j)
        act(0, nt - LAG + j)

    @pl.loop(LAG, nt)
    def _(j):
        up(2, j)
        down_load(j).start()
        c_copy(2, j - LAG).wait_recv()
        mid(2, j - LAG)
        act(1, j - LAG)

    @pl.loop(nt - LAG, nt)
    def _(j):
        c_copy(2, j).wait_recv()
        mid(2, j)
        act(1, j)

    @pl.loop(0, nt)
    def _(j):
        mid(3, j)

    @pl.loop(0, nt)
    def _(j):
        act(2, j)

    for part in range(3):
        hidden_ready(part, 0, nt)

    @pl.loop(0, nc)
    def _(n):
        down_load(n * 2).wait()
        down_load(n * 2 + 1).wait()
        down(n)
        act(3, n)

        @pl.when(n >= LAG)
        def _():
            rs_z(0, n - LAG)

    hidden_ready(3, 0, nc)

    @pl.loop(0, nc)
    def _(n):
        down_first(n)
        act(3, nc + n)

        @pl.when(n >= nc - LAG + 1)
        def _():
            rs_z(0, n - 1)

    hidden_ready(3, nc, nt)

    @pl.loop(0, nc)
    def _(n):
        down_second(n)

        @pl.when(n == 0)
        def _():
            rs_z(0, nc - 1)

        @pl.when(n >= LAG)
        def _():
            rs_z(1, n - LAG)

    @pl.loop(nc - LAG, nc)
    def _(n):
        rs_z(1, n)

    @pl.loop(0, nc)
    def _(n):
        rs_finish(n)

    for s in range(steps):
        for kind in range(7):
            gather(kind, s).wait_send()

    @pl.loop(0, nc)
    def _(n):
        for g in range(2):
            y_copy(g, n).wait_send()
            for hop in range(len(HOPS[g])):
                z_copy(g, n, hop).wait_send()

    @pl.loop(0, nt)
    def _(j):
        for ch in range(len(CHUNKS)):
            c_copy(ch, j).wait_send()
        for part in range(len(PARTS)):
            x_copy(part, j).wait_send()
            h_copy(part, j, c).wait_send()


def fused(groups, tokens, up_weight, up_bias, down_weight, down_bias, active):
    steps, share, depth = tokens.shape
    hidden = up_weight.shape[1]
    nt, nc, rows = hidden // TILE, depth // TILE, steps * groups * share
    f32, bf16 = jnp.float32, jnp.bfloat16
    any_space, vmem = pl.BlockSpec(memory_space=pl.ANY), pl.BlockSpec(memory_space=pltpu.VMEM)
    smem = pl.BlockSpec(memory_space=pltpu.SMEM)
    dma = pltpu.SemaphoreType.DMA
    half = TILE // 2
    mixed = pl.pallas_call(
        functools.partial(fused_kernel, nt),
        out_shape=jax.ShapeDtypeStruct(tokens.shape, f32),
        in_specs=[any_space, any_space, any_space, vmem, smem],
        out_specs=vmem,
        scratch_shapes=[
            pltpu.VMEM((rows, depth), bf16),
            pltpu.VMEM((nt, depth, TILE), bf16),
            pltpu.VMEM((nt, 2, rows, half), f32),
            pltpu.VMEM((nt, rows, half), f32),
            pltpu.VMEM((nt, rows, half), bf16),
            pltpu.VMEM((nt, rows, half), bf16),
            pltpu.VMEM((rows, hidden), bf16),
            pltpu.VMEM((rows, depth), f32),
        ]
        + [pltpu.VMEM((nc, len(PAIRS[g]), share, TILE), bf16) for g in (0, 0, 1, 1)]
        + [pltpu.VMEM((nc, len(PAIRS[g]) - 1, share, TILE), bf16) for g in (0, 0, 1, 1)]
        + [
            dma((steps,)),
            dma((nt,)),
            dma((steps, 7)),
            dma((steps, 7)),
        ]
        + [dma((len(CHUNKS) * nt,))] * 2
        + [dma((len(PARTS) * nt,))] * 4
        + [dma((2 * nc,))] * 2
        + [dma((2 * nc * 3,))] * 2,
        compiler_params=pltpu.CompilerParams(
            collective_id=0, has_side_effects=True, vmem_limit_bytes=67043328
        ),
    )(tokens, up_weight, down_weight, up_bias, active)
    return (mixed + down_bias.astype(f32)).astype(bf16)


def solution(mesh):
    placed = (
        P(None, "dp", "tensor"),
        P("tensor", "dp"),
        P("dp"),
        P("dp", "tensor"),
        P("tensor"),
        P(None, None, "dp"),
    )
    groups, columns = mesh.shape["dp"], mesh.shape["tensor"]

    def body(*args):
        steps, share, depth = args[0].shape
        hidden, table = args[1].shape[1], args[5].shape
        if (
            (groups, columns, steps, table[1]) == (8, 4, 2, 1)
            and share % 16 == 0
            and depth % TILE == 0
            and hidden == 2 * depth
            and table[2] % (hidden // TILE * 2) == 0
            and depth // TILE > LAG
        ):
            return fused(groups, *args)
        return local(*args)

    return jax.shard_map(
        body, mesh=mesh, in_specs=placed, out_specs=P(None, "dp", "tensor"), check_vma=False
    )
```

time: 84.2 us -> 78.1 us (0.928)
  Pallas kernels: 80.9 us -> 74.8 us
    pallas_call x1, Pallas kernels: 80.9 us -> 74.8 us  [fused(): pl.pallas_call(functools.partial(fused_kernel, nt), out_shape=jax.ShapeDt...]
where the time goes in v1:
time: 78.1 us; the launch traced here: 77.8 us
  Pallas kernels  74.8 us (96%)
  other arithmetic  2.99 us (4%)
    pallas_call x1, Pallas kernels, fused(): pl.pallas_call(functools.partial(fused_kernel, nt), out_shape=jax.ShapeDt...  74.8 us
    convert_element_type x2, other arithmetic, fused(): return (mixed + down_bias.astype(f32)).astype(bf16)  2.99 us

profile of v1, /device:TPU:0, one launch (start us, length us, event | category | flops | bytes accessed | tf_op | source)
XLA Modules:
  0.0 77.8 jit_solution(16949109722523722577)
XLA Ops:
  0.0 1.3 %convert_element_type.6 = f32[3072]{0:T(1024)} convert(bf16[3072]{0:T(1024)(128)(2,1)} %param.10) | non-fusion elementwise | flops 3072 | bytes 18432 | tf_op jit(solution)/shard_map/convert_element_type | solution.py:452
  1.3 74.8 %shard_map.64 = f32[2,16,3072]{2,1,0:T(8,128)} custom-call(bf16[2,16,3072]{2,1,0:T(8,128)(2,1)} %tok.1, bf16[3072,6144]{1,0:T(8,128)(2,1)} %wu.1, bf16[6144,3072]{1,0:T(8,128)(2,1)} %wd.1, bf16[6144]{0:T(1024)(128)(2,1)} %bias_u.1, s32[2,1,48]{2,1,0:T(1,128)} %active.1), custom_call_target="tpu_custom_call" | custom-call | tf_op jit(solution)/shard_map/pallas_call | solution.py:421
  76.1 1.7 %add_convert_fusion = bf16[2,16,3072]{2,1,0:T(8,128)(2,1)} fusion(f32[2,16,3072]{2,1,0:T(8,128)} %shard_map.64, f32[3072]{0:T(1024)} %convert_element_type.6), kind=kLoop, calls=%fused_computation | loop fusion | flops 196608 | bytes 602112 | tf_op jit(solution)/shard_map/convert_element_type | solution.py:452

commit v2 on v1

--- a/solution.py
+++ b/solution.py
@@ -66,7 +66,7 @@
 HOPS = (((1, 0, 1), (2, 1, 2), (3, 2, 4)), ((1, 0, 1), (2, 1, 2)))
 
 
-def fused_kernel(nt, tok, wu, wd, bias_u, active, out,
+def fused_kernel(nt, tok, wu, wd, bias_u, bias_d, active, out,
                  x_all, w, pbuf, crecv, xsend, xrecv, hid, acc,
                  ysend0, yrecv0, ysend1, yrecv1, zsend0, zrecv0, zsend1, zrecv1,
                  tsem, wsem, ag_send, ag_recv, c_send, c_recv, x_send, x_recv, h_send, h_recv,
@@ -239,17 +239,30 @@
         for hop in range(len(HOPS[g])):
             z_copy(g, n, hop).start()
 
-    def rs_finish(n):
-        for g in range(2):
-            for hop in range(len(HOPS[g])):
-                z_copy(g, n, hop).wait_recv()
-        for s in range(steps):
-            total = acc[slot(0, 0, s), cols(n)] + yrecv[s][n, 0].astype(f32)
-            for g in range(2):
-                for p, (k, step) in enumerate(PAIRS[g]):
-                    if k and step == s:
-                        total += zrecv[g][n, p - 1].astype(f32)
-            out[s, :, cols(n)] = total
+    def collect(n, g, s):
+        total = acc[slot(0, 0, s), cols(n)]
+        for p, (k, step) in enumerate(PAIRS[g]):
+            if step == s:
+                total += (zrecv[g][n, p - 1] if k else yrecv[g][n, p]).astype(f32)
+        return total
+
+    def rs_finish(g, n):
+        for hop in range(len(HOPS[g])):
+            z_copy(g, n, hop).wait_recv()
+        if g == 0:
+            acc[slot(0, 0, 1), cols(n)] = collect(n, 0, 1)
+        total = collect(n, g, g) + bias_d[cols(n)].astype(f32).reshape(1, TILE)
+        out[g, :, cols(n)] = total.astype(bf16)
+        y_copy(g, n).wait_send()
+        for hop in range(len(HOPS[g])):
+            z_copy(g, n, hop).wait_send()
+
+    def sent(j, chunks, parts):
+        for ch in chunks:
+            c_copy(ch, j).wait_send()
+        for part in parts:
+            x_copy(part, j).wait_send()
+            h_copy(part, j, c).wait_send()
 
     for copy in mine:
         copy.wait()
@@ -342,6 +355,10 @@
     def _(j):
         act(2, j)
 
+    for s in range(steps):
+        for kind in range(7):
+            gather(kind, s).wait_send()
+
     for part in range(3):
         hidden_ready(part, 0, nt)
 
@@ -351,6 +368,8 @@
         down_load(n * 2 + 1).wait()
         down(n)
         act(3, n)
+        for i in range(2):
+            sent(n * 2 + i, (0, 1), (0, 1))
 
         @pl.when(n >= LAG)
         def _():
@@ -362,6 +381,8 @@
     def _(n):
         down_first(n)
         act(3, nc + n)
+        for i in range(2):
+            sent(n * 2 + i, (2,), (2,))
 
         @pl.when(n >= nc - LAG + 1)
         def _():
@@ -372,6 +393,8 @@
     @pl.loop(0, nc)
     def _(n):
         down_second(n)
+        for i in range(2):
+            sent(n * 2 + i, (), (3,))
 
         @pl.when(n == 0)
         def _():
@@ -385,28 +408,8 @@
     def _(n):
         rs_z(1, n)
 
-    @pl.loop(0, nc)
-    def _(n):
-        rs_finish(n)
-
-    for s in range(steps):
-        for kind in range(7):
-            gather(kind, s).wait_send()
-
-    @pl.loop(0, nc)
-    def _(n):
-        for g in range(2):
-            y_copy(g, n).wait_send()
-            for hop in range(len(HOPS[g])):
-                z_copy(g, n, hop).wait_send()
-
-    @pl.loop(0, nt)
-    def _(j):
-        for ch in range(len(CHUNKS)):
-            c_copy(ch, j).wait_send()
-        for part in range(len(PARTS)):
-            x_copy(part, j).wait_send()
-            h_copy(part, j, c).wait_send()
+    for g in range(2):
+        pl.loop(0, nc)(functools.partial(rs_finish, g))
 
 
 def fused(groups, tokens, up_weight, up_bias, down_weight, down_bias, active):
@@ -418,10 +421,10 @@
     smem = pl.BlockSpec(memory_space=pltpu.SMEM)
     dma = pltpu.SemaphoreType.DMA
     half = TILE // 2
-    mixed = pl.pallas_call(
+    return pl.pallas_call(
         functools.partial(fused_kernel, nt),
-        out_shape=jax.ShapeDtypeStruct(tokens.shape, f32),
-        in_specs=[any_space, any_space, any_space, vmem, smem],
+        out_shape=jax.ShapeDtypeStruct(tokens.shape, bf16),
+        in_specs=[any_space, any_space, any_space, vmem, vmem, smem],
         out_specs=vmem,
         scratch_shapes=[
             pltpu.VMEM((rows, depth), bf16),
@@ -448,8 +451,7 @@
         compiler_params=pltpu.CompilerParams(
             collective_id=0, has_side_effects=True, vmem_limit_bytes=67043328
         ),
-    )(tokens, up_weight, down_weight, up_bias, active)
-    return (mixed + down_bias.astype(f32)).astype(bf16)
+    )(tokens, up_weight, down_weight, up_bias, down_bias, active)
 
 
 def solution(mesh):

time: 78.1 us -> 76.2 us (0.976)
  other arithmetic: 2.99 us -> 0 us
  local copies, waits for them, and re-layouts: 0 us -> 1.62 us
    convert_element_type x2 -> x0, other arithmetic: 2.99 us -> none  [fused(): return (mixed + down_bias.astype(f32)).astype(bf16)]
    unnamed x0 -> x1, local copies, waits for them, and re-layouts: none -> 1.62 us
where the time goes in v2:
time: 76.2 us; the launch traced here: 76 us
  Pallas kernels  74.3 us (98%)
  local copies, waits for them, and re-layouts  1.62 us (2%)
    pallas_call x1, Pallas kernels, fused(): pl.pallas_call(functools.partial(fused_kernel, nt), out_shape=jax.ShapeDt...  74.3 us
    unnamed x1, local copies, waits for them, and re-layouts  1.62 us

profile of v2, /device:TPU:0, one launch (start us, length us, event | category | flops | bytes accessed | tf_op | source)
XLA Modules:
  0.0 76.0 jit_solution(13489435104763880165)
XLA Ops:
  0.0 74.3 %shard_map.64 = bf16[2,16,3072]{2,1,0:T(8,128)(2,1)} custom-call(bf16[2,16,3072]{2,1,0:T(8,128)(2,1)} %tok.1, bf16[3072,6144]{1,0:T(8,128)(2,1)} %wu.1, bf16[6144,3072]{1,0:T(8,128)(2,1)} %wd.1, bf16[6144]{0:T(1024)(128)(2,1)} %bias_u.1, bf16[3072]{0:T(1024)(128)(2,1)} %bias_d.1, s32[2,1,48]{2,1,0:T(1,128)} %active.1), custom_call_target="tpu_custom_call" | custom-call | tf_op jit(solution)/shard_map/pallas_call | solution.py:424
  74.4 1.6 %copy.8 = bf16[2,16,3072]{2,1,0:T(8,128)(2,1)} copy(bf16[2,16,3072]{2,1,0:T(8,128)(2,1)} %shard_map.64) | data formatting | bytes 393216
